TPU v7x, 32 devices: a whole 2x2x4 slice. The times are simulated.
32 devices in a mesh: dom: 8 (over z, x), feat: 4 (over y, core).
Axes of the slice: x: 2, y: 2, z: 4, core: 2. Of those that a mesh axis runs over, the one named last changes fastest.
Arguments:
- node_feats: bfloat16 [16384, 512], P('dom', 'feat'), may hold values from -6 to 6
- edge_tiles: bfloat16 [848, 128, 128], P('dom'), may hold values from -0.14941406 to 0.14941406
- tile_dst: int32 [848], P('dom'), may hold values from 0 to 15, as said below
- tile_src: int32 [848], P('dom'), may hold values from 0 to 25, as said below
- hub_ids: int32 [256], P('dom'), may hold values from 0 to 2047, as said below
- send_rows: int32 [8, 8, 128], P('dom'), may hold values from 0 to 2047
- send_count: int32 [8, 8], P('dom'), may hold values from 32 to 128, as said below
- w_self: bfloat16 [512, 512], P(None, 'feat'), may hold values from -0.25 to 0.25
- w_neigh: bfloat16 [512, 512], P(None, 'feat'), may hold values from -0.25 to 0.25
- out_bias: float32 [512], P('feat'), may hold values from -3 to 3
- grad_out: bfloat16 [16384, 512], P('dom', 'feat'), may hold values from -6 to 6
Outputs:
- output: bfloat16 [16384, 512], P('dom', 'feat')
- grad_feats: float32 [16384, 512], P('dom', 'feat')
- grad_self: float32 [512, 512], P(None, 'feat')
- grad_neigh: float32 [512, 512], P(None, 'feat')
- grad_bias: float32 [512], P('feat')
Inputs may be any that keep to these rules, and one draw needn't show every extreme that they name: `tile_dst`: every one of the 16 blocks of a partition receives at least 5 of its tiles. `tile_src`: source blocks of a partition: its own rows, then all hub rows, then received rows in order of sender; every block is read by at least one tile of every partition. `hub_ids`: distinct within each partition. `send_count`: every partition sends exactly 128 rows to at least one partition, and some partition receives exactly 128 rows from every partition.
All inputs are finite; a program needn't handle non-finite values.
Results may differ from a plain program's by a relative error of at most 0.0055.
Values may be sent and summed in bfloat16 or wider, within the bound.
No kernel may reach another device: no remote copies, remote signals or barrier semaphores. Data moves between devices by JAX's collectives and lax.ppermute only.
A program may use at most 128 MiB of HBM per device.

v0:
```python
import jax
import jax.numpy as jnp
from jax import lax
from jax.sharding import PartitionSpec as P


def body(
    node_feats,
    edge_tiles,
    tile_dst,
    tile_src,
    hub_ids,
    send_rows,
    send_count,
    w_self,
    w_neigh,
    out_bias,
    grad_out,
):
    own_count, width = node_feats.shape
    tile_size = edge_tiles.shape[1]
    peer_count, capacity = (send_rows.shape[1], send_rows.shape[2])
    hub_local = node_feats[hub_ids]
    hub_table = lax.all_gather(hub_local, "dom", axis=0, tiled=True)
    listed = send_rows[0]
    filled = jnp.arange(capacity, dtype=jnp.int32)[None, :] < send_count[0][:, None]
    outgoing = jnp.where(filled[:, :, None], node_feats[listed], jnp.zeros((), node_feats.dtype))
    incoming = lax.all_to_all(outgoing, "dom", split_axis=0, concat_axis=0, tiled=True)
    source = jnp.concatenate(
        [node_feats, hub_table, incoming.reshape(peer_count * capacity, width)], axis=0
    )
    source_blocks = source.shape[0] // tile_size
    row_blocks = own_count // tile_size
    blocks = source.reshape(source_blocks, tile_size, width)
    products = jnp.einsum(
        "tij,tjf->tif", edge_tiles, blocks[tile_src], preferred_element_type=jnp.float32
    )
    summed = jax.ops.segment_sum(products, tile_dst, row_blocks)
    aggregated = summed.reshape(own_count, width).astype(jnp.bfloat16)
    whole_feats, whole_agg = (
        lax.all_gather(node_feats, "feat", axis=1, tiled=True),
        lax.all_gather(aggregated, "feat", axis=1, tiled=True),
    )
    pre_act = (
        jnp.dot(whole_feats, w_self, preferred_element_type=jnp.float32)
        + jnp.dot(whole_agg, w_neigh, preferred_element_type=jnp.float32)
        + out_bias
    )
    gate_sig = jax.nn.sigmoid(pre_act)
    output = (pre_act * gate_sig).astype(jnp.bfloat16)
    grad_pre = (
        grad_out.astype(jnp.float32) * gate_sig * (1.0 + pre_act * (1.0 - gate_sig))
    ).astype(jnp.bfloat16)
    contract_rows = (((0,), (0,)), ((), ()))
    grad_self = lax.dot_general(
        whole_feats, grad_pre, contract_rows, preferred_element_type=jnp.float32
    )
    grad_neigh = lax.dot_general(
        whole_agg, grad_pre, contract_rows, preferred_element_type=jnp.float32
    )
    grad_bias = jnp.sum(grad_pre.astype(jnp.float32), axis=0)
    grad_self, grad_neigh, grad_bias = lax.psum((grad_self, grad_neigh, grad_bias), "dom")
    contract_last = (((1,), (1,)), ((), ()))
    first = lax.dot_general(w_self, grad_pre, contract_last, preferred_element_type=jnp.float32)
    second = lax.dot_general(w_neigh, grad_pre, contract_last, preferred_element_type=jnp.float32)
    shares = lax.psum_scatter(
        jnp.concatenate([first, second], axis=1), "feat", scatter_dimension=0, tiled=True
    )
    direct = shares[:, :own_count].T
    back_agg = shares[:, own_count:].T.astype(jnp.bfloat16)
    back_blocks = back_agg.reshape(row_blocks, tile_size, width)[tile_dst]
    spread = jnp.einsum("tji,tjf->tif", edge_tiles, back_blocks, preferred_element_type=jnp.float32)
    back_source = jax.ops.segment_sum(spread, tile_src, source_blocks).reshape(-1, width)
    hub_total = hub_table.shape[0]
    hub_part = back_source[own_count : own_count + hub_total]
    recv_part = back_source[own_count + hub_total :].reshape(peer_count, capacity, width)
    hub_back = lax.psum_scatter(hub_part, "dom", scatter_dimension=0, tiled=True)
    sent_back = lax.all_to_all(
        recv_part.astype(jnp.bfloat16), "dom", split_axis=0, concat_axis=0, tiled=True
    ).astype(recv_part.dtype)
    returned = jnp.where(filled[:, :, None], sent_back, jnp.zeros((), jnp.float32))
    grad_feats = direct + back_source[:own_count]
    grad_feats = grad_feats.at[hub_ids].add(hub_back)
    grad_feats = grad_feats.at[listed.reshape(-1)].add(
        returned.reshape(peer_count * capacity, width)
    )
    return (output, grad_feats, grad_self, grad_neigh, grad_bias)


def solution(mesh):
    in_specs = (
        P("dom", "feat"),
        P("dom", None, None),
        P("dom"),
        P("dom"),
        P("dom"),
        P("dom", None, None),
        P("dom", None),
        P(None, "feat"),
        P(None, "feat"),
        P("feat"),
        P("dom", "feat"),
    )
    out_specs = (P("dom", "feat"), P("dom", "feat"), P(None, "feat"), P(None, "feat"), P("feat"))
    return jax.shard_map(body, mesh=mesh, in_specs=in_specs, out_specs=out_specs, check_vma=False)
```

profile of v0, /device:TPU:0, one launch (start us, length us, event | category | flops | bytes accessed | tf_op | source)
XLA Modules:
  0.0 419.5 jit_solution(15320924251841132812)
XLA Ops:
  8.8 5.2 %gather_fusion.1 = bf16[1024,128]{1,0:T(8,128)(2,1)} fusion(bf16[2048,128]{1,0:T(8,128)(2,1)} %param.11, s32[1024]{0:T(1024)S(1)} %fusion.3), kind=kCustom, calls=%fused_computation.1 | custom fusion | bytes 528384 | tf_op jit(solution)/shard_map/gather | solution.py:27
  16.5 7.3 %all-to-all-start = ((bf16[8,128,128]{2,1,0:T(8,128)(2,1)}), bf16[8,128,128]{2,1,0:T(8,128)(2,1)}, u32[]{:S(2)}, u32[]{:S(2)}) async-start(bf16[8,128,128]{2,1,0:T(8,128)(2,1)} %broadcast_select_fusion), calls=%async_computation | async-start | bytes 524288 | tf_op jit(solution)/shard_map/all_to_all | solution.py:28
  25.6 31.1 %all-gather = bf16[256,128]{1,0:T(8,128)(2,1)S(1)} all-gather(bf16[32,128]{1,0:T(8,128)(2,1)S(1)} %gather_fusion), channel_id=2, replica_groups=mesh['dom'=8,'feat'=4] {'dom'}, dimensions={0}, use_global_device_ids=true | all-gather | bytes 73728 | tf_op jit(solution)/shard_map/all_gather | solution.py:24
  59.5 4.0 gather_fusion.2
  63.5 7.4 %convolution_bitcast_fusion.3 = f32[106,128,128]{1,2,0:T(8,128)} fusion(bf16[106,128,128]{2,1,0:T(8,128)(2,1)} %gather_fusion.2, bf16[106,128,128]{2,1,0:T(8,128)(2,1)S(1)} %copy-done), kind=kOutput, calls=%fused_computation.12 | convolution fusion | flops 444596224 | bytes 13893632 | tf_op jit(solution)/shard_map/tij,tjf->tif/dot_general | solution.py:35
  70.9 8.3 %copy.20 = f32[106,128,128]{2,1,0:T(8,128)} copy(f32[106,128,128]{1,2,0:T(8,128)} %convolution_bitcast_fusion.3) | data formatting | bytes 13893632 | tf_op jit(solution)/shard_map/tij,tjf->tif/dot_general | solution.py:35
  80.3 22.4 %scatter_fusion = f32[16,128,128]{2,1,0:T(8,128)} fusion(f32[16,128,128]{2,1,0:T(8,128)} %broadcast_in_dim.50, s32[106]{0:T(128)S(1)} %copy-done.6, f32[106,128,128]{2,1,0:T(8,128)} %copy.20), kind=kCustom, calls=%fused_computation.4 | custom fusion | flops 1736704 | bytes 20840872 | tf_op jit(solution)/shard_map/scatter-add | solution.py:38
  104.9 3.3 fusion.4
  108.2 20.4 %all-gather.6.cloned.1.call-done = bf16[2048,512]{1,0:T(8,128)(2,1)} async-done(((bf16[2048,128]{1,0:T(8,128)(2,1)}), bf16[2048,512]{1,0:T(8,128)(2,1)}) %all-gather.6.cloned.1.call-update) | async-done | bytes 2097168 | tf_op jit(solution)/shard_map/all_gather | solution.py:42
  128.6 3.7 convert_reduce_fusion
  132.3 2.7 convolution_bitcast_fusion
  135.0 2.8 convolution_bitcast_fusion.1
  140.4 7.7 %pad_maximum_fusion = f32[512,4096]{0,1:T(8,128)} fusion(f32[512,2048]{0,1:T(8,128)} %convolution_bitcast_fusion, f32[512,2048]{0,1:T(8,128)} %convolution_bitcast_fusion.1), kind=kLoop, calls=%fused_computation.8 | loop fusion | flops 2097152 | bytes 16777216 | tf_op jit(solution)/shard_map/concatenate | solution.py:67
  148.8 22.0 %psum.23 = f32[128]{0:T(128)} all-reduce(f32[128]{0:T(128)S(1)} %get-tuple-element.17), channel_id=1, replica_groups=mesh['dom'=8,'feat'=4] {'dom'}, use_global_device_ids=true, to_apply=%region_9.10 | all-reduce | flops 128 | bytes 1024 | tf_op jit(solution)/shard_map/psum | solution.py:62
  170.9 42.4 %all-reduce.3.cloned.1.call-done = (f32[512,128]{0,1:T(8,128)}, f32[512,128]{1,0:T(8,128)}) async-done(((f32[512,128]{0,1:T(8,128)}, f32[512,128]{1,0:T(8,128)}), (f32[512,128]{0,1:T(8,128)}, f32[512,128]{1,0:T(8,128)})) %all-reduce.3.cloned.1.call-update) | async-done | bytes 524304 | tf_op jit(solution)/shard_map/psum | solution.py:62
  215.0 71.8 %reduce-scatter.3.cloned.1.call-done = f32[128,4096]{0,1:T(8,128)} async-done(((f32[512,4096]{0,1:T(8,128)}), f32[128,4096]{0,1:T(8,128)}) %reduce-scatter.3.cloned.1.call-update) | async-done | bytes 2097168 | tf_op jit(solution)/shard_map/reduce_scatter | solution.py:66
  288.9 3.8 gather_fusion.3
  292.7 6.2 %convolution_bitcast_fusion.2 = f32[106,128,128]{1,2,0:T(8,128)} fusion(bf16[106,128,128]{2,1,0:T(8,128)(2,1)} %gather_fusion.3, bf16[106,128,128]{2,1,0:T(8,128)(2,1)S(1)} %copy-done), kind=kOutput, calls=%fused_computation.11 | convolution fusion | flops 444596224 | bytes 13893632 | tf_op jit(solution)/shard_map/tji,tjf->tif/dot_general | solution.py:72
  298.9 8.3 %copy.22 = f32[106,128,128]{2,1,0:T(8,128)} copy(f32[106,128,128]{1,2,0:T(8,128)} %convolution_bitcast_fusion.2) | data formatting | bytes 13893632 | tf_op jit(solution)/shard_map/tji,tjf->tif/dot_general | solution.py:72
  308.6 22.7 %scatter_fusion.1 = f32[26,128,128]{2,1,0:T(8,128)} fusion(f32[26,128,128]{2,1,0:T(8,128)} %broadcast_in_dim.56, s32[106]{0:T(128)S(1)} %copy-done.7, f32[106,128,128]{2,1,0:T(8,128)} %copy.22), kind=kCustom, calls=%fused_computation.5 | custom fusion | flops 1736704 | bytes 20840872 | tf_op jit(solution)/shard_map/scatter-add | solution.py:73
  337.2 5.6 %all-to-all-start.1 = ((bf16[8,128,128]{2,1,0:T(8,128)(2,1)}), bf16[8,128,128]{2,1,0:T(8,128)(2,1)}, u32[]{:S(2)}, u32[]{:S(2)}) async-start(bf16[8,128,128]{2,1,0:T(8,128)(2,1)} %slice.50), calls=%async_computation.3 | async-start | bytes 524288 | tf_op jit(solution)/shard_map/all_to_all | solution.py:78
  345.3 53.0 %reduce-scatter.5.cloned.1.call-done = f32[32,128]{1,0:T(8,128)} async-done(((f32[256,128]{1,0:T(8,128)}), f32[32,128]{1,0:T(8,128)}) %reduce-scatter.5.cloned.1.call-update) | async-done | bytes 16400 | tf_op jit(solution)/shard_map/reduce_scatter | solution.py:77
  398.3 3.1 scatter_fusion.2
  403.3 8.0 %scatter_fusion.3 = f32[2048,128]{1,0:T(8,128)} fusion(f32[2048,128]{1,0:T(8,128)} %scatter_fusion.2, s32[1024]{0:T(1024)S(1)} %bitcast.56, f32[1024,128]{1,0:T(8,128)} %bitcast.53), kind=kCustom, calls=%fused_computation.7 | custom fusion | flops 131072 | bytes 1576960 | tf_op jit(solution)/shard_map/scatter-add | solution.py:84
  (58 shorter events, 32.6 us)
Async XLA Ops:
  7.2 56.3 %copy-start = (bf16[106,128,128]{2,1,0:T(8,128)(2,1)S(1)}, bf16[106,128,128]{2,1,0:T(8,128)(2,1)}, u32[]{:S(2)}) copy-start(bf16[106,128,128]{2,1,0:T(8,128)(2,1)} %param.12) | copy-start | bytes 10420228
  7.2 16.7 %copy-start.8 = (s32[32]{0:T(128)S(1)}, s32[32]{0:T(128)}, u32[]{:S(2)}) copy-start(s32[32]{0:T(128)} %param.15) | copy-start | bytes 388
  7.2 97.7 %all-gather.4.cloned.1.call-start = ((), (), s32[]{:S(2)}) async-start(), calls=%async_computation.4 | async-start | bytes 2621440 | tf_op jit(solution)/shard_map/all_gather | solution.py:41
  16.5 40.8 %all-to-all-start = ((bf16[8,128,128]{2,1,0:T(8,128)(2,1)}), bf16[8,128,128]{2,1,0:T(8,128)(2,1)}, u32[]{:S(2)}, u32[]{:S(2)}) async-start(bf16[8,128,128]{2,1,0:T(8,128)(2,1)} %broadcast_select_fusion), calls=%async_computation | async-start | bytes 524288 | tf_op jit(solution)/shard_map/all_to_all | solution.py:28
  23.8 104.8 %all-gather.6.cloned.1.call-start = ((), (), s32[]{:S(2)}) async-start(), calls=%async_computation.5 | async-start | bytes 2621440 | tf_op jit(solution)/shard_map/all_gather | solution.py:42
  70.9 9.4 %copy-start.6 = (s32[106]{0:T(128)S(1)}, s32[106]{0:T(128)}, u32[]{:S(2)}) copy-start(s32[106]{0:T(128)} %param.13) | copy-start | bytes 1276
  102.7 25.9 %copy-start.9 = (f32[128]{0:T(128)S(1)}, f32[128]{0:T(128)}, u32[]{:S(2)}) copy-start(f32[128]{0:T(128)} %param.20) | copy-start | bytes 1540
  104.8 108.4 %all-reduce.3.cloned.1.call-start = ((), (), s32[]{:S(2)}) async-start(), calls=%async_computation.8 | async-start | bytes 1048576 | tf_op jit(solution)/shard_map/psum | solution.py:62
  128.6 3.7 copy-start.4
  132.3 2.7 copy-start.3
  135.0 2.8 copy-start.2
  135.0 4.2 %copy-start.1 = (bf16[2048,512]{1,0:T(8,128)(2,1)S(1)}, bf16[2048,512]{1,0:T(8,128)(2,1)}, u32[]{:S(2)}) copy-start(bf16[2048,512]{1,0:T(8,128)(2,1)} %all-gather.4.cloned.1.call-done) | copy-start | bytes 6291460
  140.4 146.4 %reduce-scatter.3.cloned.1.call-start = ((), (), s32[]{:S(2)}) async-start(), calls=%async_computation.6 | async-start | bytes 10485760 | tf_op jit(solution)/shard_map/reduce_scatter | solution.py:66
  148.1 0.7 copy-start.5
  148.2 250.1 %reduce-scatter.5.cloned.1.call-start = ((), (), s32[]{:S(2)}) async-start(), calls=%async_computation.7 | async-start | bytes 147456 | tf_op jit(solution)/shard_map/reduce_scatter | solution.py:77
  298.9 9.7 %copy-start.7 = (s32[106]{0:T(128)S(1)}, s32[106]{0:T(128)}, u32[]{:S(2)}) copy-start(s32[106]{0:T(128)} %param.14) | copy-start | bytes 1276
  337.2 64.2 %all-to-all-start.1 = ((bf16[8,128,128]{2,1,0:T(8,128)(2,1)}), bf16[8,128,128]{2,1,0:T(8,128)(2,1)}, u32[]{:S(2)}, u32[]{:S(2)}) async-start(bf16[8,128,128]{2,1,0:T(8,128)(2,1)} %slice.50), calls=%async_computation.3 | async-start | bytes 524288 | tf_op jit(solution)/shard_map/all_to_all | solution.py:78
Sparse Core Ops, SparseCore 0:
  9.6 25.5 all-gather.3
  105.0 23.6 all-gather.5
  140.5 72.6 all-reduce.2
  215.8 70.9 reduce-scatter.2
  337.3 60.9 reduce-scatter.4
where the time goes:
time: 421 us; the launch traced here: 420 us
  waiting for transfers between devices  188 us (45%)
  other arithmetic  76.7 us (18%)
  blocking collectives  53.2 us (13%)
  local copies, waits for them, and re-layouts  45.8 us (11%)
  matrix products  28.6 us (7%)
  between operations  13.9 us (3%)
  starting transfers between devices  13 us (3%)
    reduce_scatter x1, waiting for transfers between devices, body(): lax.psum_scatter(jnp.concatenate([first, second], axis=1), 'feat', scatte...  71.8 us
    reduce_scatter x1, waiting for transfers between devices, body(): lax.psum_scatter(hub_part, 'dom', scatter_dimension=0, tiled=True)  53 us
    psum x1, waiting for transfers between devices, body(): lax.psum((grad_self, grad_neigh, grad_bias), 'dom')  42.4 us
    all_gather x1, blocking collectives, body(): hub_table = lax.all_gather(hub_local, 'dom', axis=0, tiled=True)  31.1 us
    scatter-add x1, other arithmetic, body(): jax.ops.segment_sum(spread, tile_src, source_blocks).reshape(-1, width)  22.7 us
    scatter-add x1, other arithmetic, body(): summed = jax.ops.segment_sum(products, tile_dst, row_blocks)  22.4 us
    psum x1, blocking collectives, body(): lax.psum((grad_self, grad_neigh, grad_bias), 'dom')  22 us
    all_gather x1, waiting for transfers between devices, body(): lax.all_gather(aggregated, 'feat', axis=1, tiled=True)  20.4 us
  transfers between devices with their start and end apart: 7, of which 4 were waited for; matrix products, arithmetic and copies ran while one was open for 18% of the time, Pallas kernels for 0%

commit v1 on v0

--- a/solution.py
+++ b/solution.py
@@ -21,7 +21,15 @@
     tile_size = edge_tiles.shape[1]
     peer_count, capacity = (send_rows.shape[1], send_rows.shape[2])
     hub_local = node_feats[hub_ids]
-    hub_table = lax.all_gather(hub_local, "dom", axis=0, tiled=True)
+    ways, here = (lax.axis_size("dom"), lax.axis_index("dom"))
+    grown, reach = (hub_local, 1)
+    while reach < ways:
+        theirs = lax.ppermute(grown, "dom", [(d, d ^ reach) for d in range(ways)])
+        mine_first = jnp.concatenate([grown, theirs], axis=0)
+        theirs_first = jnp.concatenate([theirs, grown], axis=0)
+        grown = jnp.where(here & reach == 0, mine_first, theirs_first)
+        reach = 2 * reach
+    hub_table = grown
     listed = send_rows[0]
     filled = jnp.arange(capacity, dtype=jnp.int32)[None, :] < send_count[0][:, None]
     outgoing = jnp.where(filled[:, :, None], node_feats[listed], jnp.zeros((), node_feats.dtype))

time: 421 us -> 403 us (0.957)
  blocking collectives: 53.2 us -> 22 us
  starting transfers between devices: 13 us -> 18.8 us
  waiting for transfers between devices: 188 us -> 193 us
    all_gather x1 -> x0, blocking collectives: 31.1 us -> none  [body(): hub_table = lax.all_gather(hub_local, 'dom', axis=0, tiled=True)]
    ppermute x0 -> x3, starting transfers between devices: none -> 8.14 us  [body(): theirs = lax.ppermute(grown, 'dom', [(d, d ^ reach) for d in range(ways)])]
    ppermute x0 -> x3, waiting for transfers between devices: none -> 4.68 us  [body(): theirs = lax.ppermute(grown, 'dom', [(d, d ^ reach) for d in range(ways)])]
  transfers between devices with their start and end apart: 7 -> 10, of which waited for: 4 -> 6; matrix products, arithmetic and copies ran while one was open for 18% -> 20% of each run, Pallas kernels for 0% -> 0%
where the time goes in v1:
time: 403 us; the launch traced here: 401 us
  waiting for transfers between devices  193 us (48%)
  other arithmetic  78.9 us (20%)
  local copies, waits for them, and re-layouts  45.7 us (11%)
  matrix products  28.6 us (7%)
  blocking collectives  22 us (5%)
  starting transfers between devices  18.8 us (5%)
  between operations  13.9 us (3%)
    reduce_scatter x1, waiting for transfers between devices, body(): lax.psum_scatter(jnp.concatenate([first, second], axis=1), 'feat', scatte...  71.8 us
    reduce_scatter x1, waiting for transfers between devices, body(): lax.psum_scatter(hub_part, 'dom', scatter_dimension=0, tiled=True)  53 us
    psum x1, waiting for transfers between devices, body(): lax.psum((grad_self, grad_neigh, grad_bias), 'dom')  42.4 us
    scatter-add x1, other arithmetic, body(): jax.ops.segment_sum(spread, tile_src, source_blocks).reshape(-1, width)  22.9 us
    scatter-add x1, other arithmetic, body(): summed = jax.ops.segment_sum(products, tile_dst, row_blocks)  22.4 us
    psum x1, blocking collectives, body(): lax.psum((grad_self, grad_neigh, grad_bias), 'dom')  22 us
    all_gather x1, waiting for transfers between devices, body(): lax.all_gather(aggregated, 'feat', axis=1, tiled=True)  20.2 us
    dot_general x1, local copies, waits for them, and re-layouts, body(): jnp.einsum('tij,tjf->tif', edge_tiles, blocks[tile_src], preferred_elemen...  8.35 us
  transfers between devices with their start and end apart: 10, of which 6 were waited for; matrix products, arithmetic and copies ran while one was open for 20% of the time, Pallas kernels for 0%

profile of v1, /device:TPU:0, one launch (start us, length us, event | category | flops | bytes accessed | tf_op | source)
XLA Modules:
  0.0 400.8 jit_solution(10952055561778916014)
XLA Ops:
  10.4 3.0 collective-permute-start
  14.1 5.2 %gather_fusion.1 = bf16[1024,128]{1,0:T(8,128)(2,1)} fusion(bf16[2048,128]{1,0:T(8,128)(2,1)} %param.11, s32[1024]{0:T(1024)S(1)} %fusion.3), kind=kCustom, calls=%fused_computation.1 | custom fusion | bytes 528384 | tf_op jit(solution)/shard_map/gather | solution.py:35
  21.9 4.9 %all-to-all-start = ((bf16[8,128,128]{2,1,0:T(8,128)(2,1)}), bf16[8,128,128]{2,1,0:T(8,128)(2,1)}, u32[]{:S(2)}, u32[]{:S(2)}) async-start(bf16[8,128,128]{2,1,0:T(8,128)(2,1)} %broadcast_select_fusion), calls=%async_computation | async-start | bytes 524288 | tf_op jit(solution)/shard_map/all_to_all | solution.py:36
  29.4 3.3 collective-permute-done.1
  32.8 3.1 collective-permute-start.2
  40.8 4.0 %gather_fusion.2 = bf16[106,128,128]{2,1,0:T(8,128)(2,1)} fusion(bf16[26,128,128]{2,1,0:T(8,128)(2,1)} %bitcast.51, s32[1024]{0:T(1024)S(1)} %pad_clamp_fusion.1), kind=kCustom, calls=%fused_computation.2 | custom fusion | bytes 6947240 | tf_op jit(solution)/shard_map/gather | solution.py:44
  44.8 7.4 %convolution_bitcast_fusion.3 = f32[106,128,128]{1,2,0:T(8,128)} fusion(bf16[106,128,128]{2,1,0:T(8,128)(2,1)} %gather_fusion.2, bf16[106,128,128]{2,1,0:T(8,128)(2,1)S(1)} %copy-done), kind=kOutput, calls=%fused_computation.12 | convolution fusion | flops 444596224 | bytes 13893632 | tf_op jit(solution)/shard_map/tij,tjf->tif/dot_general | solution.py:43
  52.3 8.4 %copy.20 = f32[106,128,128]{2,1,0:T(8,128)} copy(f32[106,128,128]{1,2,0:T(8,128)} %convolution_bitcast_fusion.3) | data formatting | bytes 13893632 | tf_op jit(solution)/shard_map/tij,tjf->tif/dot_general | solution.py:43
  61.7 22.4 %scatter_fusion = f32[16,128,128]{2,1,0:T(8,128)} fusion(f32[16,128,128]{2,1,0:T(8,128)} %broadcast_in_dim.50, s32[106]{0:T(128)S(1)} %copy-done.7, f32[106,128,128]{2,1,0:T(8,128)} %copy.20), kind=kCustom, calls=%fused_computation.4 | custom fusion | flops 1736704 | bytes 20840872 | tf_op jit(solution)/shard_map/scatter-add | solution.py:46
  86.3 3.3 fusion.4
  89.6 20.2 %all-gather.5.cloned.1.call-done = bf16[2048,512]{1,0:T(8,128)(2,1)} async-done(((bf16[2048,128]{1,0:T(8,128)(2,1)}), bf16[2048,512]{1,0:T(8,128)(2,1)}) %all-gather.5.cloned.1.call-update) | async-done | bytes 2097168 | tf_op jit(solution)/shard_map/all_gather | solution.py:50
  109.8 3.7 convert_reduce_fusion
  121.6 7.7 %pad_maximum_fusion = f32[512,4096]{0,1:T(8,128)} fusion(f32[512,2048]{0,1:T(8,128)} %convolution_bitcast_fusion, f32[512,2048]{0,1:T(8,128)} %convolution_bitcast_fusion.1), kind=kLoop, calls=%fused_computation.8 | loop fusion | flops 2097152 | bytes 16777216 | tf_op jit(solution)/shard_map/concatenate | solution.py:75
  130.0 22.0 %psum.23 = f32[128]{0:T(128)} all-reduce(f32[128]{0:T(128)S(1)} %get-tuple-element.17), channel_id=1, replica_groups=mesh['dom'=8,'feat'=4] {'dom'}, use_global_device_ids=true, to_apply=%region_9.10 | all-reduce | flops 128 | bytes 1024 | tf_op jit(solution)/shard_map/psum | solution.py:70
  152.0 42.4 %all-reduce.3.cloned.1.call-done = (f32[512,128]{0,1:T(8,128)}, f32[512,128]{1,0:T(8,128)}) async-done(((f32[512,128]{0,1:T(8,128)}, f32[512,128]{1,0:T(8,128)}), (f32[512,128]{0,1:T(8,128)}, f32[512,128]{1,0:T(8,128)})) %all-reduce.3.cloned.1.call-update) | async-done | bytes 524304 | tf_op jit(solution)/shard_map/psum | solution.py:70
  196.2 71.8 %reduce-scatter.3.cloned.1.call-done = f32[128,4096]{0,1:T(8,128)} async-done(((f32[512,4096]{0,1:T(8,128)}), f32[128,4096]{0,1:T(8,128)}) %reduce-scatter.3.cloned.1.call-update) | async-done | bytes 2097168 | tf_op jit(solution)/shard_map/reduce_scatter | solution.py:74
  270.1 3.8 gather_fusion.3
  273.9 6.2 %convolution_bitcast_fusion.2 = f32[106,128,128]{1,2,0:T(8,128)} fusion(bf16[106,128,128]{2,1,0:T(8,128)(2,1)} %gather_fusion.3, bf16[106,128,128]{2,1,0:T(8,128)(2,1)S(1)} %copy-done), kind=kOutput, calls=%fused_computation.11 | convolution fusion | flops 444596224 | bytes 13893632 | tf_op jit(solution)/shard_map/tji,tjf->tif/dot_general | solution.py:80
  280.1 8.3 %copy.22 = f32[106,128,128]{2,1,0:T(8,128)} copy(f32[106,128,128]{1,2,0:T(8,128)} %convolution_bitcast_fusion.2) | data formatting | bytes 13893632 | tf_op jit(solution)/shard_map/tji,tjf->tif/dot_general | solution.py:80
  289.8 22.9 %scatter_fusion.1 = f32[26,128,128]{2,1,0:T(8,128)} fusion(f32[26,128,128]{2,1,0:T(8,128)} %broadcast_in_dim.56, s32[106]{0:T(128)S(1)} %copy-done.8, f32[106,128,128]{2,1,0:T(8,128)} %copy.22), kind=kCustom, calls=%fused_computation.5 | custom fusion | flops 1736704 | bytes 20840872 | tf_op jit(solution)/shard_map/scatter-add | solution.py:81
  318.5 5.6 %all-to-all-start.1 = ((bf16[8,128,128]{2,1,0:T(8,128)(2,1)}), bf16[8,128,128]{2,1,0:T(8,128)(2,1)}, u32[]{:S(2)}, u32[]{:S(2)}) async-start(bf16[8,128,128]{2,1,0:T(8,128)(2,1)} %slice.50), calls=%async_computation.3 | async-start | bytes 524288 | tf_op jit(solution)/shard_map/all_to_all | solution.py:86
  326.6 53.0 %reduce-scatter.5.cloned.1.call-done = f32[32,128]{1,0:T(8,128)} async-done(((f32[256,128]{1,0:T(8,128)}), f32[32,128]{1,0:T(8,128)}) %reduce-scatter.5.cloned.1.call-update) | async-done | bytes 16400 | tf_op jit(solution)/shard_map/reduce_scatter | solution.py:85
  379.6 3.1 scatter_fusion.2
  384.6 8.0 %scatter_fusion.3 = f32[2048,128]{1,0:T(8,128)} fusion(f32[2048,128]{1,0:T(8,128)} %scatter_fusion.2, s32[1024]{0:T(1024)S(1)} %bitcast.56, f32[1024,128]{1,0:T(8,128)} %bitcast.53), kind=kCustom, calls=%fused_computation.7 | custom fusion | flops 131072 | bytes 1576960 | tf_op jit(solution)/shard_map/scatter-add | solution.py:92
  (66 shorter events, 43.4 us)
Async XLA Ops:
  7.2 37.7 %copy-start = (bf16[106,128,128]{2,1,0:T(8,128)(2,1)S(1)}, bf16[106,128,128]{2,1,0:T(8,128)(2,1)}, u32[]{:S(2)}) copy-start(bf16[106,128,128]{2,1,0:T(8,128)(2,1)} %param.12) | copy-start | bytes 10420228
  7.2 21.7 %copy-start.8 = (s32[106]{0:T(128)S(1)}, s32[106]{0:T(128)}, u32[]{:S(2)}) copy-start(s32[106]{0:T(128)} %param.14) | copy-start | bytes 1276
  7.2 79.1 %all-gather.3.cloned.1.call-start = ((), (), s32[]{:S(2)}) async-start(), calls=%async_computation.4 | async-start | bytes 2621440 | tf_op jit(solution)/shard_map/all_gather | solution.py:49
  10.4 16.4 %collective-permute-start = (bf16[32,128]{1,0:T(8,128)(2,1)S(1)}, bf16[32,128]{1,0:T(8,128)(2,1)S(1)}, u32[]{:S(2)}, u32[]{:S(2)}) collective-permute-start(bf16[32,128]{1,0:T(8,128)(2,1)S(1)} %gather_fusion), channel_id=1, source_target_pairs={{0,4},{4,0},{8,12},{12,8},{16,20},{20,16},{24,28},{28,24},{1,5},{5... | collective-permute-start | bytes 24584 | tf_op jit(solution)/shard_map/ppermute | solution.py:27
  21.9 16.8 %all-to-all-start = ((bf16[8,128,128]{2,1,0:T(8,128)(2,1)}), bf16[8,128,128]{2,1,0:T(8,128)(2,1)}, u32[]{:S(2)}, u32[]{:S(2)}) async-start(bf16[8,128,128]{2,1,0:T(8,128)(2,1)} %broadcast_select_fusion), calls=%async_computation | async-start | bytes 524288 | tf_op jit(solution)/shard_map/all_to_all | solution.py:36
  26.8 83.0 %all-gather.5.cloned.1.call-start = ((), (), s32[]{:S(2)}) async-start(), calls=%async_computation.5 | async-start | bytes 2621440 | tf_op jit(solution)/shard_map/all_gather | solution.py:50
  26.9 5.9 %collective-permute-start.1 = (bf16[64,128]{1,0:T(8,128)(2,1)S(1)}, bf16[64,128]{1,0:T(8,128)(2,1)S(1)}, u32[]{:S(2)}, u32[]{:S(2)}) collective-permute-start(bf16[64,128]{1,0:T(8,128)(2,1)S(1)} %maximum_select_fusion.2), channel_id=1, source_target_pairs={{0,8},{4,12},{8,0},{12,4},{16,24},{20,28},{24,16},{28,20},{1,9},{5... | collective-permute-start | bytes 49160 | tf_op jit(solution)/shard_map/ppermute | solution.py:27
  32.7 3.8 copy-start.5
  32.8 5.1 %collective-permute-start.2 = (bf16[128,128]{1,0:T(8,128)(2,1)S(1)}, bf16[128,128]{1,0:T(8,128)(2,1)}, u32[]{:S(2)}, u32[]{:S(2)}) collective-permute-start(bf16[128,128]{1,0:T(8,128)(2,1)S(1)} %maximum_select_fusion.1), channel_id=1, source_target_pairs={{0,16},{4,20},{8,24},{12,28},{16,0},{20,4},{24,8},{28,12},{1,17},{... | collective-permute-start | bytes 98312 | tf_op jit(solution)/shard_map/ppermute | solution.py:27
  52.3 9.4 %copy-start.7 = (s32[106]{0:T(128)S(1)}, s32[106]{0:T(128)}, u32[]{:S(2)}) copy-start(s32[106]{0:T(128)} %param.13) | copy-start | bytes 1276
  84.1 25.7 %copy-start.9 = (f32[128]{0:T(128)S(1)}, f32[128]{0:T(128)}, u32[]{:S(2)}) copy-start(f32[128]{0:T(128)} %param.20) | copy-start | bytes 1540
  86.2 108.2 %all-reduce.3.cloned.1.call-start = ((), (), s32[]{:S(2)}) async-start(), calls=%async_computation.8 | async-start | bytes 1048576 | tf_op jit(solution)/shard_map/psum | solution.py:70
  109.8 3.7 copy-start.4
  113.5 2.7 copy-start.3
  116.1 2.8 copy-start.2
  116.1 4.2 %copy-start.1 = (bf16[2048,512]{1,0:T(8,128)(2,1)S(1)}, bf16[2048,512]{1,0:T(8,128)(2,1)}, u32[]{:S(2)}) copy-start(bf16[2048,512]{1,0:T(8,128)(2,1)} %all-gather.3.cloned.1.call-done) | copy-start | bytes 6291460
  121.5 146.4 %reduce-scatter.3.cloned.1.call-start = ((), (), s32[]{:S(2)}) async-start(), calls=%async_computation.6 | async-start | bytes 10485760 | tf_op jit(solution)/shard_map/reduce_scatter | solution.py:74
  129.3 0.7 copy-start.6
  129.3 250.3 %reduce-scatter.5.cloned.1.call-start = ((), (), s32[]{:S(2)}) async-start(), calls=%async_computation.7 | async-start | bytes 147456 | tf_op jit(solution)/shard_map/reduce_scatter | solution.py:85
  318.5 64.2 %all-to-all-start.1 = ((bf16[8,128,128]{2,1,0:T(8,128)(2,1)}), bf16[8,128,128]{2,1,0:T(8,128)(2,1)}, u32[]{:S(2)}, u32[]{:S(2)}) async-start(bf16[8,128,128]{2,1,0:T(8,128)(2,1)} %slice.50), calls=%async_computation.3 | async-start | bytes 524288 | tf_op jit(solution)/shard_map/all_to_all | solution.py:86
Sparse Core Ops, SparseCore 0:
  9.6 25.5 all-gather.2
  86.3 23.4 all-gather.4
  121.7 72.7 all-reduce.2
  197.0 70.9 reduce-scatter.2
  318.6 60.9 reduce-scatter.4
